TPU v7x, 128 devices: a whole 4x4x4 slice. The times are simulated.
128 devices in a mesh: expert: 32 (over y, z, core), vocab: 4 (over x).
Axes of the slice: x: 4, y: 4, z: 4, core: 2. Of those that a mesh axis runs over, the one named last changes fastest.
Arguments:
- tokens: bfloat16 [4096, 2048], P('expert'), may hold values from -12 to 12
- expert_ids: int32 [4096, 6], P('expert'), may hold values from 0 to 63, all different within a row; in each aligned block of 128 rows (0 to 127, 128 to 255, ...) at most 24 rows name the same one
- gates: float32 [4096, 6], P('expert'), may hold values from 0.05 to 0.4
- w_gate: bfloat16 [64, 2048, 1408], P('expert', None, 'vocab'), may hold values from -0.125 to 0.125
- w_up: bfloat16 [64, 2048, 1408], P('expert', None, 'vocab'), may hold values from -0.125 to 0.125
- w_down: bfloat16 [64, 1408, 2048], P('expert', 'vocab'), may hold values from -0.21875 to 0.21875
- norm_gain: float32 [2048], replicated, may hold values from 0.5 to 1.5
- lm_weight: bfloat16 [2048, 98304], P(None, ('expert', 'vocab')), may hold values from -6.9605824 to 6.9605824
- targets: int32 [4096], P('expert'), may hold values from 0 to 98303
Outputs:
- logprobs: float32 [4096], P('expert')
Inputs may be any that keep to these rules, and one draw needn't show every extreme that they name: `expert_ids`: in the 128 rows of one device no expert is named by more than 24 routes; each row names 6 different experts.
All inputs are finite; a program needn't handle non-finite values.
Results may differ from a plain program's by a relative error of at most 0.003.
Values may be sent and summed in bfloat16 or wider, within the bound.
A program may use at most 128 MiB of HBM per device.

v0:
```python
import jax
import jax.numpy as jnp
from jax import lax
from jax.sharding import PartitionSpec as P


def split_up(array, dim, count):
    before, after = (array.shape[:dim], array.shape[dim + 1 :])
    return jnp.moveaxis(array.reshape(*before, count, -1, *after), dim, 0)


def piece_ends(length, count):
    unit = 8 if length >= 8 * count else 1
    return [length // unit * k // count * unit for k in range(1, count)]


def laid_out(parts, dim):
    shape = list(parts.shape[1:])
    shape[dim] *= parts.shape[0]
    return jnp.moveaxis(parts, 0, dim).reshape(shape)


def several_exchanges(array, axis, pieces, split_dim, concat_dim):
    parts = split_up(array, split_dim, lax.axis_size(axis))
    widest = max(range(1, max(2, parts.ndim - 1)), key=lambda d: parts.shape[d])
    done = []
    for share in jnp.split(parts, piece_ends(parts.shape[widest], pieces), axis=widest):
        if share.size:
            done.append(lax.all_to_all(share, axis, split_axis=0, concat_axis=0, tiled=True))
    return laid_out(jnp.concatenate(done, axis=widest), concat_dim)


def copy_for_each(array, axis):
    count = lax.axis_size(axis)
    return lax.all_to_all(
        jnp.broadcast_to(array[None], (count, *array.shape)), axis, 0, 0, tiled=True
    )


def taken_together(array, axis):
    everything = copy_for_each(array, axis)
    return jnp.sum(everything, axis=0)


def gathered_once(array, axis):
    leaves = jax.tree.leaves(array)
    turns = sorted(range(len(leaves)), key=lambda k: -leaves[k].size)
    width = (1, *leaves[turns[0]].shape)[-1]
    lines = [
        jnp.pad(leaves[k].reshape(-1), (0, -leaves[k].size % width)).reshape(-1, width)
        for k in turns
    ]
    both, at, found = (copy_for_each(jnp.concatenate(lines), axis), 0, {})
    for k, line in zip(turns, lines):
        share = both[:, at : at + len(line)].reshape(len(both), -1)
        found[k] = share[:, : leaves[k].size].reshape(-1, *leaves[k].shape)
        at += len(line)
    numbers = iter(range(len(leaves)))
    return jax.tree.map(lambda _: found[next(numbers)], array)


def joined_by_halves(pieces, combine):
    while len(jax.tree.leaves(pieces)[0]) > 1:
        pieces = jax.vmap(combine)(
            *(jax.tree.map(lambda part: part[side::2], pieces) for side in (0, 1))
        )
    return jax.tree.map(lambda part: part[0], pieces)


def joined_all(array, axis, combine):
    pieces = gathered_once(array, axis)
    return joined_by_halves(pieces, combine)


def expert_rows(received, w_gate, w_up, w_down):
    groups = w_gate.shape[0]
    shaped = received.reshape(-1, groups, received.shape[1], received.shape[2])
    gate_val = jnp.einsum("sltd,ldf->sltf", shaped, w_gate, preferred_element_type=jnp.float32)
    up_val = jnp.einsum("sltd,ldf->sltf", shaped, w_up, preferred_element_type=jnp.float32)
    hidden = (jax.nn.silu(gate_val) * up_val).astype(jnp.bfloat16)
    result = jnp.einsum("sltf,lfd->sltd", hidden, w_down, preferred_element_type=jnp.float32)
    return result.reshape(received.shape[0], received.shape[1], result.shape[3])


def shard_stats(logits, row_targets, base):
    columns = base + jnp.arange(logits.shape[1], dtype=jnp.int32)
    top_now = jnp.max(logits, axis=1)
    total_now = jnp.sum(jnp.exp(logits - top_now[:, None]), axis=1)
    picked_now = jnp.sum(jnp.where(columns[None, :] == row_targets[:, None], logits, 0.0), axis=1)
    return (top_now, total_now, picked_now)


def join_stats(first, second):
    best = jnp.maximum(first[0], second[0])
    mass = first[1] * jnp.exp(first[0] - best) + second[1] * jnp.exp(second[0] - best)
    return (best, mass, first[2] + second[2])


def body(tokens, expert_ids, gates, w_gate, w_up, w_down, norm_gain, lm_weight, targets):
    tok_rows = tokens.shape[0]
    top_count = expert_ids.shape[1]
    groups = w_gate.shape[0]
    width = tokens.shape[1]
    expert_devs = lax.axis_size("expert")
    vocab_devs = lax.axis_size("vocab")
    experts_all = groups * expert_devs
    slots = 2 * tok_rows * top_count // experts_all
    vocab_index = lax.axis_index("vocab")
    flat_ids = expert_ids.reshape(-1)
    onehot = (flat_ids[:, None] == jnp.arange(experts_all, dtype=jnp.int32)[None, :]).astype(
        jnp.int32
    )
    slot_ids = jnp.sum((jnp.cumsum(onehot, axis=0) - onehot) * onehot, axis=1)
    target_rows = (flat_ids * slots + slot_ids).reshape(tok_rows, top_count)
    places = jnp.arange(experts_all * slots, dtype=jnp.int32)
    packed = jnp.dot(
        jnp.any(places[:, None, None] == target_rows[None, :, :], axis=2).astype(jnp.bfloat16),
        tokens,
        preferred_element_type=jnp.float32,
    ).astype(jnp.bfloat16)
    packed = packed.reshape(experts_all, slots, width)
    partial_value = expert_rows(
        lax.all_to_all(packed, "expert", split_axis=0, concat_axis=0, tiled=True),
        w_gate,
        w_up,
        w_down,
    )
    combined = several_exchanges(partial_value, "expert", 2, 0, 0)
    flat_back = combined.reshape(experts_all * slots, combined.shape[2])
    picked = jnp.take(flat_back, target_rows.reshape(-1), axis=0).reshape(
        tok_rows, top_count, flat_back.shape[1]
    )
    mixture = jnp.sum(picked * gates[:, :, None], axis=1)
    base = (lax.axis_index("expert") * vocab_devs + vocab_index) * lm_weight.shape[1]
    mixture = taken_together(mixture, "vocab")
    resid = (tokens.astype(jnp.float32) + mixture).astype(jnp.bfloat16)
    resid_f = resid.astype(jnp.float32)
    squares = jnp.mean(resid_f * resid_f, axis=1)
    normed = (resid_f * lax.rsqrt(squares + 1e-06)[:, None] * norm_gain[None, :]).astype(
        jnp.bfloat16
    )
    rows = lax.all_gather(normed, "expert", axis=0, tiled=True)
    row_targets = lax.all_gather(targets, "expert", axis=0, tiled=True)
    logits = jnp.dot(rows, lm_weight, preferred_element_type=jnp.float32)
    fresh = shard_stats(logits, row_targets, base)
    top_all, total_all, chosen_all = tuple((new for new in fresh))
    top_got, total_got, chosen_got = (
        lax.all_to_all(top_all, "expert", split_axis=0, concat_axis=0, tiled=True),
        lax.all_to_all(total_all, "expert", split_axis=0, concat_axis=0, tiled=True),
        lax.all_to_all(chosen_all, "expert", split_axis=0, concat_axis=0, tiled=True),
    )
    top_got = top_got.reshape(expert_devs, tok_rows)
    total_got = total_got.reshape(expert_devs, tok_rows)
    chosen_got = chosen_got.reshape(expert_devs, tok_rows)
    best = jnp.max(top_got, axis=0)
    mass = jnp.sum(total_got * jnp.exp(top_got - best[None, :]), axis=0)
    chosen = jnp.sum(chosen_got, axis=0)
    best, mass, chosen = joined_all((best, mass, chosen), "vocab", join_stats)
    return chosen - best - jnp.log(mass)


def solution(mesh):
    in_specs = (
        P("expert", None),
        P("expert", None),
        P("expert", None),
        P("expert", None, "vocab"),
        P("expert", None, "vocab"),
        P("expert", "vocab", None),
        P(),
        P(None, ("expert", "vocab")),
        P("expert"),
    )
    out_specs = P("expert")
    return jax.shard_map(body, mesh=mesh, in_specs=in_specs, out_specs=out_specs, check_vma=False)
```

profile of v0, /device:TPU:0, one launch (start us, length us, event | category | flops | bytes accessed | tf_op | source)
XLA Modules:
  0.0 552.3 jit_solution(4479632245104566551)
XLA Ops:
  14.6 81.5 %all_to_all.52 = bf16[64,24,2048]{2,1,0:T(8,128)(2,1)S(1)} all-to-all(bf16[64,24,2048]{2,1,0:T(8,128)(2,1)S(1)} %bitcast.93), channel_id=1, replica_groups=mesh['expert'=32,'vocab'=4] {'expert'}, dimensions={0} | all-to-all | bytes 12582912 | tf_op jit(solution)/shard_map/all_to_all | solution.py:123
  98.7 4.9 fusion.2
  103.5 13.6 %convolution_bitcast_fusion = f32[32,2,24,2048]{3,2,0,1:T(8,128)} fusion(bf16[2,352,2048]{2,1,0:T(8,128)(2,1)} %param.14, f32[2,32,24,352]{3,2,1,0:T(8,128)} %fusion.2, bf16[2,2048,352]{1,2,0:T(8,128)(2,1)} %param.13, bf16[32,2,24,2048]{3,2,1,0:T(8,128)(2,1)} %bitcast.95), kind=kOutput, calls=%fused_computation.10 | convolution fusion | flops 4432429056 | bytes 26804224 | tf_op jit(solution)/shard_map/sltf,lfd->sltd/dot_general | solution.py:81
  121.5 4.9 all-to-all-start.1
  129.8 3.8 copy.55
  133.6 45.4 %all-to-all-done.1 = f32[32,2,8,2048]{3,2,1,0:T(8,128)} async-done(((f32[32,2,8,2048]{3,2,1,0:T(8,128)}), f32[32,2,8,2048]{3,2,1,0:T(8,128)}, u32[]{:S(2)}, u32[]{:S(2)}) %all-to-all-start.1) | async-done | bytes 4194336 | tf_op jit(solution)/shard_map/all_to_all | solution.py:29
  178.9 6.8 %all-to-all-start.2 = ((f32[32,2,16,2048]{3,2,1,0:T(8,128)}), f32[32,2,16,2048]{3,2,1,0:T(8,128)}, u32[]{:S(2)}, u32[]{:S(2)}) async-start(f32[32,2,16,2048]{3,2,1,0:T(8,128)} %copy.55), calls=%async_computation.2 | async-start | bytes 16777216 | tf_op jit(solution)/shard_map/all_to_all | solution.py:29
  186.4 112.9 %all-to-all-done.2 = f32[32,2,16,2048]{3,2,1,0:T(8,128)} async-done(((f32[32,2,16,2048]{3,2,1,0:T(8,128)}), f32[32,2,16,2048]{3,2,1,0:T(8,128)}, u32[]{:S(2)}, u32[]{:S(2)}) %all-to-all-start.2) | async-done | bytes 8388640 | tf_op jit(solution)/shard_map/all_to_all | solution.py:29
  299.3 11.3 %pad_maximum_fusion = f32[32,2,24,2048]{3,2,1,0:T(8,128)} fusion(f32[32,2,16,2048]{3,2,1,0:T(8,128)} %all-to-all-done.2, f32[32,2,8,2048]{3,2,1,0:T(8,128)} %all-to-all-done.1), kind=kLoop, calls=%fused_computation.1 | loop fusion | flops 3145728 | bytes 25165824 | tf_op jit(solution)/shard_map/concatenate | solution.py:30
  310.6 11.8 %gather_fusion = f32[768,2048]{1,0:T(8,128)} fusion(f32[1536,2048]{1,0:T(8,128)} %bitcast.92, s32[1024]{0:T(1024)S(1)} %pad_clamp_fusion), kind=kCustom, calls=%fused_computation | custom fusion | bytes 12585984 | tf_op jit(solution)/shard_map/jit(_take)/gather | solution.py:130
  322.4 7.8 %gather.7 = f32[128,6,2048]{2,1,0:T(8,128)} reshape(f32[768,2048]{1,0:T(8,128)} %gather_fusion) | data formatting | bytes 12582912 | tf_op jit(solution)/shard_map/jit(_take)/gather | solution.py:130
  330.3 6.5 %multiply_reduce_fusion = f32[128,2048]{1,0:T(8,128)S(1)} fusion(f32[128,6,2048]{2,1,0:T(8,128)} %gather.7, f32[128,6]{1,0:T(8,128)S(1)} %copy.57, pred[128,6]{1,0:T(8,128)(4,1)S(1)} %copy.51), kind=kLoop, calls=%fused_computation.4 | loop fusion | flops 4456448 | bytes 7343872 | tf_op jit(solution)/shard_map/reduce_sum | solution.py:133
  337.3 47.0 %all_to_all.53 = f32[4,128,2048]{2,1,0:T(8,128)} all-to-all(f32[4,128,2048]{2,1,0:T(8,128)S(1)} %broadcast_in_dim.20), channel_id=1, replica_groups=mesh['expert'=32,'vocab'=4] {'vocab'}, dimensions={0} | all-to-all | bytes 8388608 | tf_op jit(solution)/shard_map/all_to_all | solution.py:35
  384.3 3.6 reduce_sum.80
  391.9 37.4 %all-gather = s32[32,1,128]{2,1,0:T(1,128)S(1)} all-gather(s32[1,1,128]{2,1,0:T(1,128)S(1)} %bitcast.109), channel_id=1, replica_groups=mesh['expert'=32,'vocab'=4] {'expert'}, dimensions={0}, use_global_device_ids=true | all-gather | bytes 16896 | tf_op jit(solution)/shard_map/all_gather | solution.py:143
  429.3 47.4 %all-gather.3.cloned.1.call-done = bf16[4096,2048]{1,0:T(8,128)(2,1)} async-done(((bf16[128,2048]{1,0:T(8,128)(2,1)}), bf16[4096,2048]{1,0:T(8,128)(2,1)}) %all-gather.3.cloned.1.call-update) | async-done | bytes 16777232 | tf_op jit(solution)/shard_map/all_gather | solution.py:142
  476.7 20.1 %fusion.33 = (f32[4096]{0:T(1024)}, f32[4096,768]{0,1:T(8,128)}) fusion(bf16[4096,2048]{1,0:T(8,128)(2,1)} %all-gather.3.cloned.1.call-done, bf16[2048,768]{1,0:T(8,128)(2,1)S(1)} %copy-done), kind=kOutput, calls=%fused_computation.55 | convolution fusion | flops 12888043520 | bytes 32522240 | tf_op jit(solution)/shard_map/dot_general | solution.py:144
  496.8 5.4 all-to-all-start.4
  502.2 7.2 %exponential_reduce_fusion = (f32[4096]{0:T(1024)}, f32[4096]{0:T(1024)}) fusion(f32[4096,768]{0,1:T(8,128)} %get-tuple-element.15, f32[4096]{0:T(1024)} %get-tuple-element.14, s32[4096]{0:T(1024)S(1)} %bitcast.97, s32[768]{0:T(1024)S(1)} %iota_add_fusion), kind=kLoop, calls=%fused_computation.3 | loop fusion | flops 15720448 | bytes 12651520 | tf_op jit(solution)/shard_map/reduce_sum | solution.py:88
  509.6 7.2 %all-to-all-start.5 = ((f32[32,128,1]{1,2,0:T(1,128)}), f32[32,128,1]{1,2,0:T(1,128)S(1)}, u32[]{:S(2)}, u32[]{:S(2)}) async-start(f32[32,128,1]{1,2,0:T(1,128)} %bitcast.16), calls=%async_computation.5 | async-start | bytes 32768 | tf_op jit(solution)/shard_map/all_to_all | solution.py:149
  516.9 7.3 %all-to-all-done.5 = f32[32,128,1]{1,2,0:T(1,128)S(1)} async-done(((f32[32,128,1]{1,2,0:T(1,128)}), f32[32,128,1]{1,2,0:T(1,128)S(1)}, u32[]{:S(2)}, u32[]{:S(2)}) %all-to-all-start.5) | async-done | bytes 16416 | tf_op jit(solution)/shard_map/all_to_all | solution.py:149
  524.2 3.8 all-to-all-start.6
  528.0 7.3 %all-to-all-done.6 = f32[32,128,1]{1,2,0:T(1,128)S(1)} async-done(((f32[32,128,1]{1,2,0:T(1,128)}), f32[32,128,1]{1,2,0:T(1,128)S(1)}, u32[]{:S(2)}, u32[]{:S(2)}) %all-to-all-start.6) | async-done | bytes 16416 | tf_op jit(solution)/shard_map/all_to_all | solution.py:150
  535.4 9.4 %all_to_all.54 = f32[4,3,128]{2,1,0:T(4,128)S(1)} all-to-all(f32[4,3,128]{2,1,0:T(4,128)S(1)} %broadcast_in_dim.22), channel_id=1, replica_groups=mesh['expert'=32,'vocab'=4] {'vocab'}, dimensions={0} | all-to-all | bytes 12288 | tf_op jit(solution)/shard_map/all_to_all | solution.py:35
  (62 shorter events, 24.5 us)
Async XLA Ops:
  6.5 470.2 %copy-start = (bf16[2048,768]{1,0:T(8,128)(2,1)S(1)}, bf16[2048,768]{1,0:T(8,128)(2,1)}, u32[]{:S(2)}) copy-start(bf16[2048,768]{1,0:T(8,128)(2,1)} %param.16) | copy-start | bytes 9437188
  14.6 84.1 %copy-start.6 = (bf16[2,2048,352]{1,2,0:T(8,128)(2,1)S(1)}, bf16[2,2048,352]{1,2,0:T(8,128)(2,1)}, u32[]{:S(2)}) copy-start(bf16[2,2048,352]{1,2,0:T(8,128)(2,1)} %param.12) | copy-start | bytes 8650756
  96.1 2.6 copy-start.1
  117.1 2.2 slice-start
  121.5 57.4 %all-to-all-start.1 = ((f32[32,2,8,2048]{3,2,1,0:T(8,128)}), f32[32,2,8,2048]{3,2,1,0:T(8,128)}, u32[]{:S(2)}, u32[]{:S(2)}) async-start(f32[32,2,8,2048]{3,2,1,0:T(8,128)} %copy.54), calls=%async_computation.1 | async-start | bytes 8388608 | tf_op jit(solution)/shard_map/all_to_all | solution.py:29
  126.4 3.4 slice-start.1
  133.6 52.2 %copy-start.2 = (s32[128,6]{0,1:T(8,128)S(1)}, s32[128,6]{0,1:T(8,128)}, u32[]{:S(2)}) copy-start(s32[128,6]{0,1:T(8,128)} %param.10) | copy-start | bytes 9220
  133.6 52.7 %copy-start.4 = (f32[128,6]{0,1:T(8,128)S(1)}, f32[128,6]{0,1:T(8,128)}, u32[]{:S(2)}) copy-start(f32[128,6]{0,1:T(8,128)} %param.11) | copy-start | bytes 9220
  178.9 120.3 %all-to-all-start.2 = ((f32[32,2,16,2048]{3,2,1,0:T(8,128)}), f32[32,2,16,2048]{3,2,1,0:T(8,128)}, u32[]{:S(2)}, u32[]{:S(2)}) async-start(f32[32,2,16,2048]{3,2,1,0:T(8,128)} %copy.55), calls=%async_computation.2 | async-start | bytes 16777216 | tf_op jit(solution)/shard_map/all_to_all | solution.py:29
  185.8 290.9 %all-gather.3.cloned.1.call-start = ((), (), s32[]{:S(2)}) async-start(), calls=%async_computation.8 | async-start | bytes 17301504 | tf_op jit(solution)/shard_map/all_gather | solution.py:142
  337.3 52.2 %copy-start.3 = (f32[2048]{0:T(1024)S(1)}, f32[2048]{0:T(1024)}, u32[]{:S(2)}) copy-start(f32[2048]{0:T(1024)} %param.15) | copy-start | bytes 24580
  384.3 7.5 %copy-start.5 = (s32[128]{0:T(128)S(1)}, s32[128]{0:T(128)}, u32[]{:S(2)}) copy-start(s32[128]{0:T(128)} %param.17) | copy-start | bytes 1540
  496.8 12.8 %all-to-all-start.4 = ((f32[32,128,1]{1,2,0:T(1,128)}), f32[32,128,1]{1,2,0:T(1,128)S(1)}, u32[]{:S(2)}, u32[]{:S(2)}) async-start(f32[32,128,1]{1,2,0:T(1,128)} %bitcast.14), calls=%async_computation.4 | async-start | bytes 32768 | tf_op jit(solution)/shard_map/all_to_all | solution.py:148
  509.6 14.6 %all-to-all-start.5 = ((f32[32,128,1]{1,2,0:T(1,128)}), f32[32,128,1]{1,2,0:T(1,128)S(1)}, u32[]{:S(2)}, u32[]{:S(2)}) async-start(f32[32,128,1]{1,2,0:T(1,128)} %bitcast.16), calls=%async_computation.5 | async-start | bytes 32768 | tf_op jit(solution)/shard_map/all_to_all | solution.py:149
  524.2 11.2 %all-to-all-start.6 = ((f32[32,128,1]{1,2,0:T(1,128)}), f32[32,128,1]{1,2,0:T(1,128)S(1)}, u32[]{:S(2)}, u32[]{:S(2)}) async-start(f32[32,128,1]{1,2,0:T(1,128)} %bitcast.23), calls=%async_computation.6 | async-start | bytes 32768 | tf_op jit(solution)/shard_map/all_to_all | solution.py:150
Sparse Core Ops, SparseCore 0:
  392.0 84.6 all-gather.2
where the time goes:
time: 553 us; the launch traced here: 552 us
  waiting for transfers between devices  221 us (40%)
  blocking collectives  175 us (32%)
  matrix products  41.4 us (7%)
  local copies, waits for them, and re-layouts  36.7 us (7%)
  other arithmetic  36.7 us (7%)
  starting transfers between devices  28.1 us (5%)
  between operations  13.6 us (2%)
    all_to_all x2, waiting for transfers between devices, several_exchanges(): lax.all_to_all(share, axis, split_axis=0, concat_axis=0, tiled=True)  158 us
    all_to_all x1, blocking collectives, body(): lax.all_to_all(packed, 'expert', split_axis=0, concat_axis=0, tiled=True)  81.5 us
    all_to_all x2, blocking collectives, copy_for_each(): lax.all_to_all(jnp.broadcast_to(array[None], (count, *array.shape)), axis...  56.4 us
    all_gather x1, waiting for transfers between devices, body(): rows = lax.all_gather(normed, 'expert', axis=0, tiled=True)  47.4 us
    all_gather x1, blocking collectives, body(): row_targets = lax.all_gather(targets, 'expert', axis=0, tiled=True)  37.4 us
    dot_general x1, matrix products, body(): logits = jnp.dot(rows, lm_weight, preferred_element_type=jnp.float32)  20.1 us
    gather x2, local copies, waits for them, and re-layouts, body(): jnp.take(flat_back, target_rows.reshape(-1), axis=0)  19.6 us
    dot_general x1, matrix products, expert_rows(): jnp.einsum('sltf,lfd->sltd', hidden, w_down, preferred_element_type=jnp.f...  13.6 us
  transfers between devices with their start and end apart: 6, of which 6 were waited for; matrix products, arithmetic and copies ran while one was open for 2% of the time, Pallas kernels for 0%

commit v1 on v0

v1 whole, which is shorter than its diff:
```python
import jax
import jax.numpy as jnp
from jax import lax
from jax.experimental import pallas as pl
from jax.experimental.pallas import tpu as pltpu
from jax.sharding import PartitionSpec as P

MESH = pl.DeviceIdType.MESH
BF = jnp.bfloat16
F32 = jnp.float32
COLORS = (("x", "y", "z", 0, 768), ("y", "z", "x", 768, 640), ("z", "x", "y", 1408, 640))


def coords():
    e = lax.axis_index("expert")
    return {"x": lax.axis_index("vocab"), "y": e // 8, "z": (e // 2) % 4, "c": e % 2}


def device(co, **changed):
    q = dict(co, **changed)
    return {"expert": (q["y"] * 4 + q["z"]) * 2 + q["c"], "vocab": q["x"]}


def shift(co, dim, by):
    return (co[dim] + by) % 4


def view(buf, idx, cols, half=None):
    rows = slice(None) if half is None else pl.ds(16 * half, 16)
    y, z, x = (pl.ds(0, 4) if idx[d] is None else idx[d] for d in "yzx")
    return buf.at[y, z, x, rows, pl.ds(cols[0], cols[1])]


def remote(src, dst, ssem, rsem, to):
    return pltpu.make_async_remote_copy(src, dst, ssem, rsem, device_id=to, device_id_type=MESH)


class GatherRing:
    def __init__(self, buf, co, dim, idx, cols, ssem, rsem):
        self.buf, self.co, self.dim, self.idx, self.cols = buf, co, dim, idx, cols
        self.ssem, self.rsem = ssem, rsem
        self.left, self.right = shift(co, dim, -1), shift(co, dim, 1)
        self.far, self.me = shift(co, dim, 2), co[dim]

    def copy(self, n, k, half, to):
        ref = view(self.buf, dict(self.idx, **{self.dim: k}), self.cols, half)
        return remote(ref, ref, self.ssem.at[n], self.rsem.at[n], device(self.co, **{self.dim: to}))

    def start(self):
        self.copy(0, self.me, None, self.right).start()
        self.copy(1, self.me, None, self.left).start()

    def forward(self):
        self.copy(0, self.left, None, self.right).wait_recv()
        self.copy(2, self.left, 0, self.right).start()
        self.copy(1, self.right, None, self.left).wait_recv()
        self.copy(3, self.right, 1, self.left).start()

    def forward_left(self):
        self.copy(0, self.left, None, self.right).wait_recv()
        self.copy(2, self.left, 0, self.right).start()

    def forward_right(self):
        self.copy(1, self.right, None, self.left).wait_recv()
        self.copy(3, self.right, 1, self.left).start()

    def finish(self):
        self.copy(2, self.far, 0, self.right).wait_recv()
        self.copy(3, self.far, 1, self.left).wait_recv()

    def drain(self):
        self.copy(0, self.me, None, self.right).wait_send()
        self.copy(1, self.me, None, self.left).wait_send()
        self.copy(2, self.left, 0, self.right).wait_send()
        self.copy(3, self.right, 1, self.left).wait_send()


def gather_all(buf, co, ssem, rsem):
    first, second, third = [], [], []
    for n, (a, b, c, lo, width) in enumerate(COLORS):
        base = {d: co[d] for d in "xyz"}
        first.append(GatherRing(buf, co, a, base, (lo, width), ssem.at[n, 0], rsem.at[n, 0]))
        line = dict(base, **{a: None})
        second.append(GatherRing(buf, co, b, line, (lo, width), ssem.at[n, 1], rsem.at[n, 1]))
        third.append(
            [
                GatherRing(buf, co, c, dict(line, **{b: shift(co, b, k)}), (lo, width), ssem.at[n, 2 + j], rsem.at[n, 2 + j])
                for j, k in enumerate((0, -1, 1, 2))
            ]
        )
    three = range(3)
    for n in three:
        first[n].start()
    for n in three:
        first[n].forward()
    for n in three:
        first[n].finish()
        second[n].start()
        third[n][0].start()
    for n in three:
        second[n].forward_left()
        third[n][1].start()
        second[n].forward_right()
        third[n][2].start()
    for n in three:
        third[n][0].forward()
    for n in three:
        second[n].finish()
        third[n][3].start()
    for j in (1, 2):
        for n in three:
            third[n][j].forward()
    for n in three:
        third[n][0].finish()
    for n in three:
        third[n][3].forward()
    for j in (1, 2, 3):
        for n in three:
            third[n][j].finish()
    for n in three:
        for ring in [first[n], second[n]] + third[n]:
            ring.drain()


class ScatterRing:
    def __init__(self, acc, land, co, dim, idx, cols, ssem, rsem):
        self.acc, self.co, self.dim, self.idx, self.cols = acc, co, dim, idx, cols
        self.land, self.ssem, self.rsem = land, ssem, rsem
        self.left, self.right = shift(co, dim, -1), shift(co, dim, 1)
        self.far, self.me = shift(co, dim, 2), co[dim]

    def piece(self, k, half=None):
        return view(self.acc, dict(self.idx, **{self.dim: k}), self.cols, half)

    def landing(self, n):
        cols = pl.ds(self.cols[0], self.cols[1])
        full = [slice(None)] * (len(self.land.shape) - 3)
        if n < 2:
            return self.land.at[(0, *full, pl.ds(16 * n, 16), cols)]
        return self.land.at[(n - 1, *full, slice(None), cols)]

    def copy(self, n, src, to):
        return remote(src, self.landing(n), self.ssem.at[n], self.rsem.at[n], device(self.co, **{self.dim: to}))

    def add(self, k, half, n):
        at, got = self.piece(k, half), self.landing(n)
        at[...] = (at[...].astype(F32) + got[...].astype(F32)).astype(BF)

    def start(self):
        self.copy(0, self.piece(self.far, 0), self.left).start()
        self.copy(1, self.piece(self.far, 1), self.right).start()

    def forward(self):
        self.copy(0, self.piece(self.left, 0), self.left).wait_recv()
        self.add(self.left, 0, 0)
        self.copy(2, self.piece(self.left), self.left).start()
        self.copy(1, self.piece(self.right, 1), self.right).wait_recv()
        self.add(self.right, 1, 1)
        self.copy(3, self.piece(self.right), self.right).start()

    def finish(self):
        self.copy(2, self.piece(self.me), self.left).wait_recv()
        self.add(self.me, None, 2)
        self.copy(3, self.piece(self.me), self.right).wait_recv()
        self.add(self.me, None, 3)

    def drain(self):
        self.copy(0, self.piece(self.far, 0), self.left).wait_send()
        self.copy(1, self.piece(self.far, 1), self.right).wait_send()
        self.copy(2, self.piece(self.left), self.left).wait_send()
        self.copy(3, self.piece(self.right), self.right).wait_send()


def scatter_all(acc, land_c, land_b, land_a, co, ssem, rsem):
    first, second, third = [], [], []
    for n, (a, b, c, lo, width) in enumerate(COLORS):
        base = {d: co[d] for d in "xyz"}
        cols = (lo, width)
        line = dict(base, **{a: None})
        first.append(
            [
                ScatterRing(acc, land_c.at[j], co, c, dict(line, **{b: shift(co, b, k)}), cols, ssem.at[n, j], rsem.at[n, j])
                for j, k in enumerate((2, -1, 1, 0))
            ]
        )
        second.append(ScatterRing(acc, land_b, co, b, line, cols, ssem.at[n, 4], rsem.at[n, 4]))
        third.append(ScatterRing(acc, land_a, co, a, base, cols, ssem.at[n, 5], rsem.at[n, 5]))
    three = range(3)
    for j in range(4):
        for n in three:
            first[n][j].start()
    for j in range(4):
        for n in three:
            first[n][j].forward()
    for n in three:
        first[n][0].finish()
        second[n].start()
    for j in (1, 2):
        for n in three:
            first[n][j].finish()
    for n in three:
        second[n].forward()
    for n in three:
        first[n][3].finish()
    for n in three:
        second[n].finish()
        third[n].start()
    for n in three:
        third[n].forward()
    for n in three:
        third[n].finish()
    for n in three:
        for ring in first[n] + [second[n], third[n]]:
            ring.drain()


def greet(barrier, to):
    pl.semaphore_signal(barrier, inc=1, device_id=to, device_id_type=MESH)


def greet_neighbours(co, barrier):
    for dim in "xyz":
        for by in (1, -1):
            greet(barrier, device(co, **{dim: shift(co, dim, by)}))
    greet(barrier, device(co, c=1 - co["c"]))


def plane_peer(co, r):
    q = (co["y"] * 4 + co["z"] + r) % 16
    return device(co, y=q // 4, z=q % 4)


def experts_kernel(
    tok, info, wg, wu, wd, part, info_all,
    buf, vg, vu, vd, rows, picks, row_gate, masks, gates, places,
    ssem, rsem, isend, irecv, wsend, wrecv, local,
):
    co = coords()
    q_me = co["y"] * 4 + co["z"]
    barrier = pltpu.get_barrier_semaphore()
    greet_neighbours(co, barrier)
    for r in range(1, 16):
        greet(barrier, plane_peer(co, r))
    own = pltpu.make_async_copy(
        tok.at[pl.ds(pl.multiple_of(co["x"] * 32, 32), 32)], buf.at[co["y"], co["z"], co["x"]], local.at[0]
    )
    own.start()
    mine = pl.ds(co["c"] * 2, 2)
    pairs = ((wg, vg), (wu, vu), (wd, vd))
    weights = [pltpu.make_async_copy(src, dst.at[mine], local.at[1 + i]) for i, (src, dst) in enumerate(pairs)]
    for w in weights:
        w.start()
    info_all[0] = info[...]
    own.wait()
    pl.semaphore_wait(barrier, 22)
    swaps = [
        remote(src, dst.at[mine], wsend.at[i], wrecv.at[i], device(co, c=1 - co["c"])) for i, (src, dst) in enumerate(pairs)
    ]
    notes = [remote(info, info_all.at[r], isend.at[r], irecv.at[r], plane_peer(co, r)) for r in range(1, 16)]
    for n in notes:
        n.start()
    for s in swaps:
        s.start()
    gather_all(buf, co, ssem, rsem)
    for n in notes:
        n.wait()

    def read_source(q, _):
        got = info_all[(q_me - q + 16) % 16]
        ids, weight = got[0:6], got[8:14]
        mask_rows, gate_rows = [], []
        for l in range(4):
            hit = ids == (4 * q_me + l).astype(F32)
            mask_rows.append(jnp.sum(jnp.where(hit, 1.0, 0.0), axis=0, keepdims=True))
            gate_rows.append(jnp.sum(jnp.where(hit, weight, 0.0), axis=0, keepdims=True))
        zero = jnp.zeros((4, 128), F32)
        at = pl.ds(pl.multiple_of(q * 8, 8), 8)
        masks[at] = jnp.concatenate(mask_rows + [zero], axis=0)
        gates[at] = jnp.concatenate(gate_rows + [zero], axis=0)
        return 0

    lax.fori_loop(0, 16, read_source, 0)
    before = (
        lax.broadcasted_iota(jnp.int32, (128, 128), 0) < lax.broadcasted_iota(jnp.int32, (128, 128), 1)
    ).astype(F32).astype(BF)
    taken = masks[...]
    ahead = jnp.dot(taken.astype(BF), before, preferred_element_type=F32)
    places[...] = jnp.where(taken > 0.0, ahead, -1.0)

    def select(p, _):
        slot = lax.broadcasted_iota(jnp.int32, (24, 128), 0).astype(F32)
        zero = jnp.zeros((24, 128), F32)
        at = pl.ds(pl.multiple_of(p * 16, 16), 16)
        place, weight = places[at], gates[at]
        out = []
        for l in range(4):
            for s in range(2):
                k = s * 8 + l
                hit = jnp.where(place[k : k + 1] == slot, 1.0, 0.0)
                out.append(jnp.concatenate([hit, zero] if s == 0 else [zero, hit], axis=1))
                row_gate[l, pl.ds(pl.multiple_of(p * 48 + s * 24, 8), 24)] = jnp.sum(
                    hit * weight[k : k + 1], axis=1, keepdims=True
                )
        pick = jnp.concatenate(out, axis=0).astype(BF)
        picks[p] = pick
        two = buf[p // 2, pl.ds((p % 2) * 2, 2)].reshape(256, 2048)
        got = jnp.dot(pick, two, preferred_element_type=F32).astype(BF)
        for l in range(4):
            rows[l, pl.ds(pl.multiple_of(p * 48, 16), 48)] = got[l * 48 : (l + 1) * 48]
        return 0

    lax.fori_loop(0, 8, select, 0)
    for w in weights:
        w.wait()
    for s in swaps:
        s.wait()

    def ffn(l, _):
        got = rows[l]
        gate = jnp.dot(got, vg[l], preferred_element_type=F32)
        up = jnp.dot(got, vu[l], preferred_element_type=F32)
        hidden = (gate / (1.0 + jnp.exp(-gate)) * up).astype(BF)
        rows[l] = (jnp.dot(hidden, vd[l], preferred_element_type=F32) * row_gate[l]).astype(BF)
        return 0

    lax.fori_loop(0, 4, ffn, 0)

    def combine(p, _):
        at = pl.ds(pl.multiple_of(p * 48, 16), 48)
        got = jnp.concatenate([rows[l, at] for l in range(4)], axis=0)
        mixed = lax.dot_general(picks[p], got, (((0,), (0,)), ((), ())), preferred_element_type=F32)
        part[p // 2, pl.ds((p % 2) * 2, 2)] = mixed.astype(BF).reshape(2, 4, 32, 2048)
        return 0

    lax.fori_loop(0, 8, combine, 0)


def head_kernel(
    part, tok, gain, lm, targets, out,
    acc, land_c, land_b, land_a, buf, words, mine, stats, got,
    sc_send, sc_recv, ga_send, ga_recv, st_send, st_recv, wsend, wrecv, local,
):
    co = coords()
    q_me = co["y"] * 4 + co["z"]
    u_me = q_me * 4 + co["x"]
    barrier = pltpu.get_barrier_semaphore()
    greet_neighbours(co, barrier)
    load = pltpu.make_async_copy(part, acc, local.at[0])
    load.start()
    words_in = pltpu.make_async_copy(lm, words.at[co["c"]], local.at[1])
    words_in.start()
    own = pltpu.make_async_copy(tok.at[pl.ds(pl.multiple_of(co["x"] * 32, 32), 32)], mine, local.at[2])
    own.start()
    load.wait()
    own.wait()
    pl.semaphore_wait(barrier, 7)
    scatter_all(acc, land_c, land_b, land_a, co, sc_send, sc_recv)
    swap = remote(lm, words.at[co["c"]], wsend, wrecv, device(co, c=1 - co["c"]))
    swap.start()
    resid = (mine[...].astype(F32) + acc[co["y"], co["z"], co["x"]].astype(F32)).astype(BF).astype(F32)
    square = jnp.mean(resid * resid, axis=1, keepdims=True)
    buf[co["y"], co["z"], co["x"]] = (resid * lax.rsqrt(square + 1e-06) * gain[...]).astype(BF)
    gather_all(buf, co, ga_send, ga_recv)
    words_in.wait()
    swap.wait()
    lane = lax.broadcasted_iota(jnp.int32, (128, 128), 1)

    def head(p, _):
        two = buf[p // 2, pl.ds((p % 2) * 2, 2)].reshape(256, 2048)
        goal = []
        for s in range(2):
            row = targets[(q_me - (2 * p + s) + 16) % 16][14:15]
            goal.append(jnp.transpose(jnp.broadcast_to(row, (128, 128)))[:, 0:1])
        goal = jnp.concatenate(goal, axis=0).astype(jnp.int32)
        tops, logits = [], []
        for c in range(2):
            value = jnp.dot(two, words[c], preferred_element_type=F32)
            logits.append(value)
            tops.append(jnp.max(value, axis=1, keepdims=True))
        top = jnp.maximum(*tops)
        total, chosen = 0.0, 0.0
        for c in range(2):
            base = ((q_me * 2 + c) * 4 + co["x"]) * 768
            total += jnp.sum(jnp.exp(logits[c] - top), axis=1, keepdims=True)
            column = lax.broadcasted_iota(jnp.int32, (256, 768), 1)
            chosen += jnp.sum(jnp.where(column == goal - base, logits[c], 0.0), axis=1, keepdims=True)
        norm = top + jnp.log(total)
        for s in range(2):
            at = slice(s * 128, (s + 1) * 128)
            both = jnp.where(lane == 0, norm[at], jnp.where(lane == 1, chosen[at], 0.0))
            stats[2 * p + s] = jnp.transpose(both)[0:2]
        return 0

    lax.fori_loop(0, 8, head, 0)

    def note(r):
        u = (u_me + r) % 64
        q = u // 4
        to = device(co, y=q // 4, z=q % 4, x=u % 4)
        return remote(stats.at[q], got.at[r], st_send.at[r], st_recv.at[r], to)

    def send(r, _):
        note(r).start()
        return 0

    def wait(r, _):
        note(r).wait()
        return 0

    lax.fori_loop(1, 64, send, 0)
    got[0] = stats[q_me]
    lax.fori_loop(1, 64, wait, 0)
    norms = got[:, 0, :]
    best = jnp.max(norms, axis=0, keepdims=True)
    mass = jnp.sum(jnp.exp(norms - best), axis=0, keepdims=True)
    chosen = jnp.sum(got[:, 1, :], axis=0, keepdims=True)
    out[...] = chosen - best - jnp.log(mass)


def vmem(*shape, dtype=BF):
    return pltpu.VMEM(shape, dtype)


def body(tokens, expert_ids, gates, w_gate, w_up, w_down, norm_gain, lm_weight, targets):
    info = jnp.concatenate(
        [
            expert_ids.astype(F32).T,
            jnp.zeros((2, 128), F32),
            gates.T,
            targets.astype(F32)[None],
            jnp.zeros((1, 128), F32),
        ],
        axis=0,
    )
    hbm, chip = pl.BlockSpec(memory_space=pl.ANY), pl.BlockSpec(memory_space=pltpu.VMEM)
    dma = pltpu.SemaphoreType.DMA
    part, info_all = pl.pallas_call(
        experts_kernel,
        out_shape=(jax.ShapeDtypeStruct((4, 4, 4, 32, 2048), BF), jax.ShapeDtypeStruct((16, 16, 128), F32)),
        in_specs=[hbm, chip, hbm, hbm, hbm],
        out_specs=(chip, chip),
        scratch_shapes=[
            vmem(4, 4, 4, 32, 2048), vmem(4, 2048, 352), vmem(4, 2048, 352), vmem(4, 352, 2048),
            vmem(4, 384, 2048), vmem(8, 192, 256), vmem(4, 384, 1, dtype=F32),
            vmem(128, 128, dtype=F32), vmem(128, 128, dtype=F32), vmem(128, 128, dtype=F32),
            dma((3, 6, 4)), dma((3, 6, 4)), dma((16,)), dma((16,)), dma((3,)), dma((3,)), dma((4,)),
        ],
        compiler_params=pltpu.CompilerParams(collective_id=0, has_side_effects=True, vmem_limit_bytes=63 << 20),
        name="experts",
    )(tokens, info, w_gate, w_up, w_down)
    out = pl.pallas_call(
        head_kernel,
        out_shape=jax.ShapeDtypeStruct((1, 128), F32),
        in_specs=[hbm, hbm, chip, hbm, chip],
        out_specs=chip,
        scratch_shapes=[
            vmem(4, 4, 4, 32, 2048), vmem(4, 3, 4, 32, 2048), vmem(3, 4, 32, 2048), vmem(3, 32, 2048),
            vmem(4, 4, 4, 32, 2048), vmem(2, 2048, 768), vmem(32, 2048),
            vmem(16, 2, 128, dtype=F32), vmem(64, 2, 128, dtype=F32),
            dma((3, 6, 4)), dma((3, 6, 4)), dma((3, 6, 4)), dma((3, 6, 4)), dma((64,)), dma((64,)), dma, dma, dma((3,)),
        ],
        compiler_params=pltpu.CompilerParams(collective_id=1, has_side_effects=True, vmem_limit_bytes=63 << 20),
        name="head",
    )(part, tokens, norm_gain[None], lm_weight, info_all)
    return out[0]


def solution(mesh):
    in_specs = (
        P("expert", None),
        P("expert", None),
        P("expert", None),
        P("expert", None, "vocab"),
        P("expert", None, "vocab"),
        P("expert", "vocab", None),
        P(),
        P(None, ("expert", "vocab")),
        P("expert"),
    )
    return jax.shard_map(body, mesh=mesh, in_specs=in_specs, out_specs=P("expert"), check_vma=False)
```

time: 553 us -> 193 us (0.35)
  waiting for transfers between devices: 221 us -> 0 us
  Pallas kernels: 0 us -> 180 us
  blocking collectives: 175 us -> 0 us
  matrix products: 41.4 us -> 0 us
  other arithmetic: 36.7 us -> 1.57 us
  starting transfers between devices: 28.1 us -> 0 us
  local copies, waits for them, and re-layouts: 36.7 us -> 10.4 us
  between operations: 13.6 us -> 0.02 us
    pallas_call x0 -> x2, Pallas kernels: none -> 180 us  [the longest x1 111 us: body(): pl.pallas_call(head_kernel, out_shape=jax.ShapeDtypeStruct((1, 128), F32)...]
    all_to_all x5 -> x0, waiting for transfers between devices: 173 us -> none  [the longest x2 158 us: several_exchanges(): lax.all_to_all(share, axis, split_axis=0, concat_axis=0, tiled=True)]
    all_to_all x3 -> x0, blocking collectives: 138 us -> none  [the longest x1 81.5 us: body(): lax.all_to_all(packed, 'expert', split_axis=0, concat_axis=0, tiled=True)]
    all_gather x1 -> x0, waiting for transfers between devices: 47.4 us -> none  [body(): rows = lax.all_gather(normed, 'expert', axis=0, tiled=True)]
    dot_general x4 -> x0, matrix products: 41.4 us -> none  [the longest x1 20.1 us: body(): logits = jnp.dot(rows, lm_weight, preferred_element_type=jnp.float32)]
    all_gather x1 -> x0, blocking collectives: 37.4 us -> none  [body(): row_targets = lax.all_gather(targets, 'expert', axis=0, tiled=True)]
    all_to_all x5 -> x0, starting transfers between devices: 28 us -> none  [the longest x2 11.7 us: several_exchanges(): lax.all_to_all(share, axis, split_axis=0, concat_axis=0, tiled=True)]
    gather x2 -> x0, local copies, waits for them, and re-layouts: 19.6 us -> none  [body(): jnp.take(flat_back, target_rows.reshape(-1), axis=0)]
  transfers between devices with their start and end apart: 6 -> 0, of which waited for: 6 -> 0; matrix products, arithmetic and copies ran while one was open for 2% -> 0% of each run, Pallas kernels for 0% -> 0%
where the time goes in v1:
time: 193 us; the launch traced here: 192 us
  Pallas kernels  180 us (93%)
  local copies, waits for them, and re-layouts  10.4 us (5%)
    pallas_call x1, Pallas kernels, body(): pl.pallas_call(head_kernel, out_shape=jax.ShapeDtypeStruct((1, 128), F32)...  111 us
    pallas_call x1, Pallas kernels, body(): pl.pallas_call(experts_kernel, out_shape=(jax.ShapeDtypeStruct((4, 4, 4,...  69.4 us
    unnamed x5, local copies, waits for them, and re-layouts  8.55 us

profile of v1, /device:TPU:0, one launch (start us, length us, event | category | flops | bytes accessed | tf_op | source)
XLA Modules:
  0.0 192.2 jit_solution(8422368072548775190)
XLA Ops:
  0.0 0.0 copy-start
  0.0 0.8 convert_bitcast_fusion.1
  0.8 0.8 convert_bitcast_fusion
  1.6 1.9 concatenate.3.info
  3.5 4.6 %copy.10.wg = bf16[2,2048,352]{2,1,0:T(8,128)(2,1)} copy(bf16[2,2048,352]{1,2,0:T(8,128)(2,1)} %param.12) | data formatting | bytes 5767168 | tf_op args[3]
  8.1 0.0 copy-done
  8.1 2.8 %copy.11.wu = bf16[2,2048,352]{2,1,0:T(8,128)(2,1)} copy(bf16[2,2048,352]{1,2,0:T(8,128)(2,1)S(1)} %copy-done) | data formatting | bytes 5767168 | tf_op args[4]
  10.9 69.4 %experts.1 = (bf16[4,4,4,32,2048]{4,3,2,1,0:T(8,128)(2,1)}, f32[16,16,128]{2,1,0:T(8,128)}) custom-call(bf16[128,2048]{1,0:T(8,128)(2,1)} %tok.3, f32[16,128]{1,0:T(8,128)} %concatenate.3.info, bf16[2,2048,352]{2,1,0:T(8,128)(2,1)} %copy.10.wg, bf16[2,2048,352]{2,1,0:T(8,128)(2,1)} %copy.11.wu, bf16[2,352,2048]{2,1,0:T(8,128)(2,1)} %wd.1), custom_call_target="tpu_custom_call" | custom-call | tf_op jit(solution)/shard_map/experts/pallas_call | solution.py:437
  80.3 110.8 %head.1 = f32[1,128]{1,0:T(1,128)} custom-call(bf16[4,4,4,32,2048]{4,3,2,1,0:T(8,128)(2,1)} %get-tuple-element.7.part, bf16[128,2048]{1,0:T(8,128)(2,1)} %tok.3, f32[1,2048]{1,0:T(1,128)} %bitcast.7, bf16[2048,768]{1,0:T(8,128)(2,1)} %lm.1, f32[16,16,128]{2,1,0:T(8,128)} %get-tuple-element.8.targets), custom_call_target="tpu_custom_call" | custom-call | tf_op jit(solution)/shard_map/head/pallas_call | solution.py:451
  191.1 1.1 copy.13
  (2 shorter events, 0.0 us)
Async XLA Ops:
  0.0 8.1 %copy-start = (bf16[2,2048,352]{1,2,0:T(8,128)(2,1)S(1)}, bf16[2,2048,352]{1,2,0:T(8,128)(2,1)}, u32[]{:S(2)}) copy-start(bf16[2,2048,352]{1,2,0:T(8,128)(2,1)} %param.13) | copy-start | bytes 8650756

commit v2 on v0

v2 whole, which is shorter than its diff:
```python
import jax
import jax.numpy as jnp
from jax import lax
from jax.experimental import pallas as pl
from jax.experimental.pallas import tpu as pltpu
from jax.sharding import PartitionSpec as P

MESH = pl.DeviceIdType.MESH
BF = jnp.bfloat16
F32 = jnp.float32
COLORS = (("x", "y", "z", 0, 768), ("z", "y", "x", 768, 768), ("x", "z", "y", 1536, 512))
BACK = (("x", "y", "z", 0, 768), ("z", "y", "x", 768, 896), ("x", "z", "y", 1664, 384))
GROUPS = (0, -1, 1, 2)
OWN, LEFT, RIGHT, FAR = range(4)


def coords():
    e = lax.axis_index("expert")
    return {"x": lax.axis_index("vocab"), "y": e // 8, "z": (e // 2) % 4, "c": e % 2}


def device(co, **changed):
    q = dict(co, **changed)
    return {"expert": (q["y"] * 4 + q["z"]) * 2 + q["c"], "vocab": q["x"]}


def shift(co, dim, by):
    return (co[dim] + by) % 4


def view(buf, idx, cols, half=None):
    rows = slice(None) if half is None else pl.ds(16 * half, 16)
    y, z, x = (pl.ds(0, 4) if idx[d] is None else idx[d] for d in "yzx")
    return buf.at[y, z, x, rows, pl.ds(cols[0], cols[1])]


def remote(src, dst, ssem, rsem, to):
    return pltpu.make_async_remote_copy(src, dst, ssem, rsem, device_id=to, device_id_type=MESH)


class GatherRing:
    def __init__(self, buf, co, dim, idx, cols, ssem, rsem):
        self.buf, self.co, self.dim, self.idx, self.cols = buf, co, dim, idx, cols
        self.ssem, self.rsem = ssem, rsem
        self.left, self.right = shift(co, dim, -1), shift(co, dim, 1)
        self.far, self.me = shift(co, dim, 2), co[dim]

    def copy(self, n, k, half, to):
        ref = view(self.buf, dict(self.idx, **{self.dim: k}), self.cols, half)
        return remote(ref, ref, self.ssem, self.rsem.at[n], device(self.co, **{self.dim: to}))

    def start(self):
        self.copy(0, self.me, None, self.right).start()
        self.copy(1, self.me, None, self.left).start()

    def forward(self):
        self.copy(0, self.left, None, self.right).wait_recv()
        self.copy(2, self.left, 0, self.right).start()
        self.copy(1, self.right, None, self.left).wait_recv()
        self.copy(2, self.right, 1, self.left).start()

    def finish(self):
        self.copy(2, self.far, None, self.right).wait_recv()


class GatherLine(GatherRing):
    def start(self):
        for n, to in enumerate((self.right, self.left, self.far)):
            self.copy(n, self.me, None, to).start()

    def finish(self):
        for n, k in enumerate((self.left, self.right, self.far)):
            self.copy(n, k, None, self.far).wait_recv()


def drain(buf, sems, colors, co, lines):
    for n, (_, _, _, lo, width) in enumerate(colors):
        cols = pl.ds(lo, width)
        sizes = (buf.at[0, 0, pl.ds(0, 3), :, cols], buf.at[pl.ds(0, 3), :, 0, :, cols], buf.at[pl.ds(0, 3), :, :, :, cols])
        for kind in range(3):
            if kind or n in lines:
                pltpu.make_async_copy(sizes[kind], sizes[kind], sems.at[n, kind]).wait()


def gather_groups(buf, co, ssem, rsem, have_x, idle, group):
    first, second, third = [], [], []
    for n, (a, b, c, lo, width) in enumerate(COLORS):
        base = {d: co[d] for d in "xyz"}
        first.append(GatherLine(buf, co, a, base, (lo, width), ssem.at[n, 0], rsem.at[n, 0]))
        line = dict(base, **{a: None})
        second.append(GatherRing(buf, co, b, line, (lo, width), ssem.at[n, 1], rsem.at[n, 1]))
        third.append(
            [
                GatherRing(buf, co, c, dict(line, **{b: shift(co, b, k)}), (lo, width), ssem.at[n, 2], rsem.at[n, 2 + j])
                for j, k in enumerate(GROUPS)
            ]
        )
    needed = [n for n in range(3) if not (have_x and COLORS[n][0] == "x")]
    ready = [n for n in range(3) if n not in needed]
    for n in needed:
        first[n].start()
    for n in ready:
        second[n].start()
    for n in ready:
        if n < 2:
            third[n][OWN].start()
    for n in needed:
        first[n].finish()
        second[n].start()
        if n < 2:
            third[n][OWN].start()
    third[2][OWN].start()
    for n in (0, 2):
        ring = second[n]
        ring.copy(0, ring.left, None, ring.right).wait_recv()
        ring.copy(2, ring.left, 0, ring.right).start()
        third[n][LEFT].start()
        ring.copy(1, ring.right, None, ring.left).wait_recv()
        ring.copy(2, ring.right, 1, ring.left).start()
        if n == 2:
            third[n][RIGHT].start()
    third[1][OWN].forward()
    third[0][OWN].forward()
    second[1].forward()
    third[1][LEFT].start()
    third[0][RIGHT].start()
    third[1][RIGHT].start()
    third[2][OWN].forward()
    for n in (0, 2, 1):
        second[n].finish()
    third[2][FAR].start()
    for n in (0, 1):
        third[n][LEFT].forward()
        third[n][FAR].start()
    for j in (LEFT, RIGHT):
        third[2][j].forward()
    idle()
    for n in (0, 1):
        third[n][OWN].finish()
    third[2][FAR].forward()
    group(OWN)
    for n in (0, 1):
        third[n][RIGHT].forward()
    for n in (0, 1):
        third[n][LEFT].finish()

    def far_on():
        for n in (0, 1):
            third[n][FAR].forward()

    group(LEFT, far_on)
    for n in (0, 1):
        third[n][RIGHT].finish()
    group(RIGHT)
    for n in (0, 1):
        third[n][FAR].finish()
    for j in range(4):
        third[2][j].finish()
    group(FAR)
    return needed


class ScatterRing:
    def __init__(self, acc, land, co, dim, idx, cols, ssem, rsem):
        self.acc, self.co, self.dim, self.idx, self.cols = acc, co, dim, idx, cols
        self.land, self.ssem, self.rsem = land, ssem, rsem
        self.left, self.right = shift(co, dim, -1), shift(co, dim, 1)
        self.far, self.me = shift(co, dim, 2), co[dim]

    def piece(self, k, half=None):
        return view(self.acc, dict(self.idx, **{self.dim: k}), self.cols, half)

    def landing(self, n):
        cols = pl.ds(self.cols[0], self.cols[1])
        full = [slice(None)] * (len(self.land.shape) - 3)
        if n < 2:
            return self.land.at[(0, *full, pl.ds(16 * n, 16), cols)]
        return self.land.at[(n - 1, *full, slice(None), cols)]

    def copy(self, n, src, to):
        sem = self.rsem.at[min(n, 2)]
        return remote(src, self.landing(n), self.ssem, sem, device(self.co, **{self.dim: to}))

    def add(self, k, half, *numbers):
        at, parts = self.piece(k, half), [self.landing(n) for n in numbers]
        if len(at.shape) == 2:
            total = at[...].astype(F32)
            for got in parts:
                total = total + got[...].astype(F32)
            at[...] = total.astype(BF)
        else:

            def one(i, _):
                total = at[i].astype(F32)
                for got in parts:
                    total = total + got[i].astype(F32)
                at[i] = total.astype(BF)
                return 0

            lax.fori_loop(0, at.shape[0], one, 0)

    def start(self):
        self.copy(0, self.piece(self.far, 0), self.left).start()
        self.copy(1, self.piece(self.far, 1), self.right).start()

    def forward(self):
        self.copy(0, self.piece(self.left, 0), self.left).wait_recv()
        self.add(self.left, 0, 0)
        self.copy(2, self.piece(self.left), self.left).start()
        self.copy(1, self.piece(self.right, 1), self.right).wait_recv()
        self.add(self.right, 1, 1)
        self.copy(3, self.piece(self.right), self.right).start()

    def finish(self):
        cols = pl.ds(self.cols[0], self.cols[1])
        full = [slice(None)] * (len(self.land.shape) - 2)
        both = self.land.at[(pl.ds(1, 2), *full, cols)]
        pltpu.make_async_copy(both, both, self.rsem.at[2]).wait()
        self.add(self.me, None, 2, 3)


class ScatterLine(ScatterRing):
    def copy(self, n, src, to):
        land = self.land.at[n, :, pl.ds(self.cols[0], self.cols[1])]
        return remote(src, land, self.ssem, self.rsem.at[n], device(self.co, **{self.dim: to}))

    def landing(self, n):
        return self.land.at[n, :, pl.ds(self.cols[0], self.cols[1])]

    def start(self):
        for n, to in enumerate((self.right, self.left, self.far)):
            self.copy(n, self.piece(to), to).start()

    def finish(self):
        for n in range(3):
            self.copy(n, self.piece(self.me), self.far).wait_recv()
        self.add(self.me, None, 0, 1, 2)


def scatter_rings(acc, land_c, land_b, land_a, co, ssem, rsem):
    first, second, third = [], [], []
    for n, (a, b, c, lo, width) in enumerate(BACK):
        base = {d: co[d] for d in "xyz"}
        cols = (lo, width)
        line = dict(base, **{a: None})
        first.append(
            [
                ScatterRing(acc, land_c.at[j], co, c, dict(line, **{b: shift(co, b, k)}), cols, ssem.at[n, 2], rsem.at[n, 2 + j])
                for j, k in enumerate(GROUPS)
            ]
        )
        second.append(ScatterRing(acc, land_b, co, b, line, cols, ssem.at[n, 1], rsem.at[n, 1]))
        third.append(ScatterLine(acc, land_a, co, a, base, cols, ssem.at[n, 0], rsem.at[n, 0]))
    return first, second, third


def greet(barrier, to):
    pl.semaphore_signal(barrier, inc=1, device_id=to, device_id_type=MESH)


def greet_neighbours(co, barrier):
    for dim in "xyz":
        for by in (1, -1):
            greet(barrier, device(co, **{dim: shift(co, dim, by)}))
    greet(barrier, device(co, c=1 - co["c"]))


def plane_peer(co, r):
    q = (co["y"] * 4 + co["z"] + r) % 16
    return device(co, y=q // 4, z=q % 4)


def kernel(
    tok, ids, weight, targets, wg, wu, wd, gain, lm, out,
    buf, vgu, vd, info, part, land_c, land_b, land_a, words, mine, goals, stats, got,
    rows, picks, row_gate, masks, gates, places,
    ga_send, ga_recv, sc_send, sc_recv, st_send, st_recv, isend, irecv, wsend, wrecv, local,
):
    co = coords()
    q_me = co["y"] * 4 + co["z"]
    sibling = device(co, c=1 - co["c"])
    barrier = pltpu.get_barrier_semaphore()
    greet_neighbours(co, barrier)

    def greet_peer(r, _):
        greet(barrier, plane_peer(co, r))
        return 0

    lax.fori_loop(1, 16, greet_peer, 0)
    shard = pl.ds(pl.multiple_of(co["x"] * 32, 32), 32)
    owns = []
    for n, (a, _, _, lo, width) in enumerate(COLORS):
        cols = pl.ds(lo, width)
        if a == "x":
            for x in range(4):
                src, dst = tok.at[pl.ds(32 * x, 32), cols], buf.at[co["y"], co["z"], x, :, cols]
                owns.append(pltpu.make_async_copy(src, dst, local.at[6 + len(owns)]))
        else:
            src, dst = tok.at[shard, cols], buf.at[co["y"], co["z"], co["x"], :, cols]
            owns.append(pltpu.make_async_copy(src, dst, local.at[6 + len(owns)]))
    for own in owns:
        own.start()
    c2 = pl.ds(co["c"] * 2, 2)
    moves = (
        (wg, vgu.at[c2, pl.ds(0, 352)]),
        (wu, vgu.at[c2, pl.ds(352, 352)]),
        (wd, vd.at[c2]),
        (lm, words.at[co["c"]]),
    )
    loads = [pltpu.make_async_copy(src, dst, local.at[1 + i]) for i, (src, dst) in enumerate(moves)]
    again = pltpu.make_async_copy(tok.at[shard], mine, local.at[5])
    zero = jnp.zeros((2, 128), F32)
    info[0] = jnp.concatenate([ids[...].astype(F32), zero, weight[...], targets[...].astype(F32), zero[0:1]], axis=0)
    for own in owns:
        own.wait()
    for load in loads + [again]:
        load.start()
    pl.semaphore_wait(barrier, 22)
    swaps = [remote(src, dst, wsend.at[i], wrecv.at[i], sibling) for i, (src, dst) in enumerate(moves)]

    def tell(r, _):
        remote(info.at[0], info.at[r], isend, irecv, plane_peer(co, r)).start()
        return 0

    lax.fori_loop(1, 16, tell, 0)
    for s in swaps:
        s.start()
    sc_first, sc_second, sc_third = scatter_rings(part, land_c, land_b, land_a, co, sc_send, sc_recv)

    def routes():
        others = info.at[pl.ds(1, 15)]
        pltpu.make_async_copy(others, others, irecv).wait()
        pltpu.make_async_copy(others, others, isend).wait()

        def read_source(q, _):
            got_info = info[(q_me - q + 16) % 16]
            named, by = got_info[0:6], got_info[8:14]
            mask_rows, gate_rows = [], []
            for l in range(4):
                hit = named == (4 * q_me + l).astype(F32)
                mask_rows.append(jnp.sum(jnp.where(hit, 1.0, 0.0), axis=0, keepdims=True))
                gate_rows.append(jnp.sum(jnp.where(hit, by, 0.0), axis=0, keepdims=True))
            none = jnp.zeros((4, 128), F32)
            at = pl.ds(pl.multiple_of(q * 8, 8), 8)
            masks[at] = jnp.concatenate(mask_rows + [none], axis=0)
            gates[at] = jnp.concatenate(gate_rows + [none], axis=0)
            goals[q] = jnp.transpose(jnp.broadcast_to(got_info[14:15], (128, 128)))
            return 0

        lax.fori_loop(0, 16, read_source, 0)
        before = (
            lax.broadcasted_iota(jnp.int32, (128, 128), 0) < lax.broadcasted_iota(jnp.int32, (128, 128), 1)
        ).astype(F32).astype(BF)
        taken = masks[...]
        ahead = jnp.dot(taken.astype(BF), before, preferred_element_type=F32)
        places[...] = jnp.where(taken > 0.0, ahead, -1.0)

        def picking(p, _):
            slot = lax.broadcasted_iota(jnp.int32, (24, 128), 0).astype(F32)
            none = jnp.zeros((24, 128), F32)
            at = pl.ds(pl.multiple_of(p * 16, 16), 16)
            place, by = places[at], gates[at]
            pick = []
            for l in range(4):
                for s in range(2):
                    k = s * 8 + l
                    hit = jnp.where(place[k : k + 1] == slot, 1.0, 0.0)
                    pick.append(jnp.concatenate([hit, none] if s == 0 else [none, hit], axis=1))
                    row_gate[l, pl.ds(pl.multiple_of(p * 48 + s * 24, 8), 24)] = jnp.sum(
                        hit * by[k : k + 1], axis=1, keepdims=True
                    )
            picks[p] = jnp.concatenate(pick, axis=0).astype(BF)
            return 0

        lax.fori_loop(0, 8, picking, 0)
        for i in range(3):
            loads[i].wait()
            swaps[i].wait()

    def experts(j, half_way=None):
        if j not in (LEFT, FAR):
            return
        pair = (OWN, LEFT) if j == LEFT else (RIGHT, FAR)
        ys = [shift(co, "y", GROUPS[k]) for k in pair]

        def place_of(t):
            return jnp.where(t < 2, ys[0], ys[1]), t % 2

        def select(t, _):
            y, i = place_of(t)
            two = buf[y, pl.ds(2 * i, 2)].reshape(256, 2048)
            chosen = jnp.dot(picks[2 * y + i], two, preferred_element_type=F32).astype(BF)
            for l in range(4):
                rows[l, pl.ds(pl.multiple_of(t * 48, 16), 48)] = chosen[l * 48 : (l + 1) * 48]
            return 0

        lax.fori_loop(0, 4, select, 0)

        def ffn(l, _):
            both = lax.dot_general(rows[l], vgu[l], (((1,), (1,)), ((), ())), preferred_element_type=F32)
            gate, up = both[:, 0:352], both[:, 352:704]
            hidden = (gate / (1.0 + jnp.exp(-gate)) * up).astype(BF)
            scale = jnp.concatenate([row_gate[l, pl.ds(pl.multiple_of(y * 96, 8), 96)] for y in ys], axis=0)
            rows[l] = (jnp.dot(hidden, vd[l], preferred_element_type=F32) * scale).astype(BF)
            return 0

        lax.fori_loop(0, 2, ffn, 0)
        if j == LEFT:
            half_way()
        else:
            for n in (0, 1):
                sc_first[n][OWN].forward()
                sc_first[n][LEFT].forward()
        lax.fori_loop(2, 4, ffn, 0)

        def combine(t, _):
            y, i = place_of(t)
            at = pl.ds(pl.multiple_of(t * 48, 16), 48)
            shares = jnp.concatenate([rows[l, at] for l in range(4)], axis=0)
            mixed = lax.dot_general(picks[2 * y + i], shares, (((0,), (0,)), ((), ())), preferred_element_type=F32)
            part[y, pl.ds(2 * i, 2)] = mixed.astype(BF).reshape(2, 4, 32, 2048)
            return 0

        lax.fori_loop(0, 4, combine, 0)
        for n in (0, 1):
            for k in (OWN, LEFT) if j == LEFT else (FAR, RIGHT):
                sc_first[n][k].start()

    lines = gather_groups(buf, co, ga_send.at[0], ga_recv.at[0], True, routes, experts)
    drain(buf, ga_send.at[0], COLORS, co, lines)
    for j in (FAR, LEFT, RIGHT, OWN):
        sc_first[2][j].start()
    for n in (0, 1, 2):
        sc_first[n][FAR].forward()
    sc_first[2][LEFT].forward()
    for n in (0, 1):
        sc_first[n][RIGHT].forward()
    for n in (0, 1, 2):
        sc_first[n][FAR].finish()
        sc_second[n].start()
    sc_first[2][RIGHT].forward()
    sc_first[2][OWN].forward()
    for n in (0, 1, 2):
        sc_first[n][LEFT].finish()
        sc_first[n][RIGHT].finish()
        sc_second[n].forward()
    for n in (0, 1, 2):
        sc_first[n][OWN].finish()
    for n in (0, 1, 2):
        sc_second[n].finish()
        sc_third[n].start()
    for n in (0, 1, 2):
        sc_third[n].finish()
    again.wait()
    resid = (mine[...].astype(F32) + part[co["y"], co["z"], co["x"]].astype(F32)).astype(BF).astype(F32)
    square = jnp.mean(resid * resid, axis=1, keepdims=True)
    buf[co["y"], co["z"], co["x"]] = (resid * lax.rsqrt(square + 1e-06) * gain[...]).astype(BF)

    def words_ready():
        loads[3].wait()
        swaps[3].wait()
        drain(part, sc_send, BACK, co, range(3))

    def head(j, half_way=None):
        y = shift(co, "y", GROUPS[j])

        def pair(i, _):
            lane = lax.broadcasted_iota(jnp.int32, (128, 128), 1)
            column = lax.broadcasted_iota(jnp.int32, (256, 768), 1)
            two = buf[y, pl.ds(2 * i, 2)].reshape(256, 2048)
            q = 4 * y + 2 * i
            goal = jnp.concatenate([goals[q + s][:, 0:1] for s in range(2)], axis=0).astype(jnp.int32)
            logits = [jnp.dot(two, words[v], preferred_element_type=F32) for v in range(2)]
            top = jnp.maximum(*[jnp.max(value, axis=1, keepdims=True) for value in logits])
            total, chosen = 0.0, 0.0
            for v in range(2):
                base = ((q_me * 2 + v) * 4 + co["x"]) * 768
                total += jnp.sum(jnp.exp(logits[v] - top), axis=1, keepdims=True)
                chosen += jnp.sum(jnp.where(column == goal - base, logits[v], 0.0), axis=1, keepdims=True)
            norm = top + jnp.log(total)
            for s in range(2):
                at = slice(s * 128, (s + 1) * 128)
                both = jnp.where(lane == 0, norm[at], jnp.where(lane == 1, chosen[at], 0.0))
                stats[q + s] = jnp.transpose(both)[0:2]
            return 0

        if half_way is None:
            lax.fori_loop(0, 2, pair, 0)
        else:
            lax.fori_loop(0, 1, pair, 0)
            half_way()
            lax.fori_loop(1, 2, pair, 0)

    def note(j, i):
        y, z, x = shift(co, "y", GROUPS[j]), (co["z"] + i // 4) % 4, (co["x"] + i) % 4
        slot = (GROUPS[j] % 4) * 16 + i
        return remote(stats.at[4 * y + z], got.at[slot], st_send, st_recv, device(co, y=y, z=z, x=x))

    def head_and_send(j, half_way=None):
        head(j, half_way)

        def send(i, _):
            note(j, i).start()
            return 0

        lax.fori_loop(1 if j == OWN else 0, 16, send, 0)

    lines = gather_groups(buf, co, ga_send.at[1], ga_recv.at[1], False, words_ready, head_and_send)
    got[0] = stats[q_me]
    drain(buf, ga_send.at[1], COLORS, co, lines)
    others = got.at[pl.ds(1, 63)]
    pltpu.make_async_copy(others, others, st_send).wait()
    pltpu.make_async_copy(others, others, st_recv).wait()
    norms = got[:, 0, :]
    best = jnp.max(norms, axis=0, keepdims=True)
    mass = jnp.sum(jnp.exp(norms - best), axis=0, keepdims=True)
    chosen = jnp.sum(got[:, 1, :], axis=0, keepdims=True)
    out[...] = chosen - best - jnp.log(mass)


def vmem(*shape, dtype=BF):
    return pltpu.VMEM(shape, dtype)


def body(tokens, expert_ids, gates, w_gate, w_up, w_down, norm_gain, lm_weight, targets):
    hbm, chip = pl.BlockSpec(memory_space=pl.ANY), pl.BlockSpec(memory_space=pltpu.VMEM)
    dma = pltpu.SemaphoreType.DMA
    out = pl.pallas_call(
        kernel,
        out_shape=jax.ShapeDtypeStruct((1, 128), F32),
        in_specs=[hbm, chip, chip, chip, hbm, hbm, hbm, chip, hbm],
        out_specs=chip,
        scratch_shapes=[
            vmem(4, 4, 4, 32, 2048), vmem(4, 704, 2048), vmem(4, 352, 2048), vmem(16, 16, 128, dtype=F32),
            vmem(4, 4, 4, 32, 2048), vmem(4, 3, 4, 32, 2048), vmem(3, 4, 32, 2048), vmem(3, 32, 2048),
            vmem(2, 2048, 768), vmem(32, 2048), vmem(16, 128, 128, dtype=F32),
            vmem(16, 2, 128, dtype=F32), vmem(64, 2, 128, dtype=F32),
            vmem(4, 192, 2048), vmem(8, 192, 256), vmem(4, 384, 1, dtype=F32),
            vmem(128, 128, dtype=F32), vmem(128, 128, dtype=F32), vmem(128, 128, dtype=F32),
            dma((2, 3, 3)), dma((2, 3, 6, 3)), dma((3, 3)), dma((3, 6, 3)), dma, dma,
            dma, dma, dma((4,)), dma((4,)), dma((15,)),
        ],
        compiler_params=pltpu.CompilerParams(collective_id=0, has_side_effects=True, vmem_limit_bytes=67043328),
        name="layer",
    )(
        tokens, expert_ids.T, gates.T, targets[None], jnp.swapaxes(w_gate, 1, 2), jnp.swapaxes(w_up, 1, 2), w_down,
        norm_gain[None], lm_weight,
    )
    return out[0]


def solution(mesh):
    in_specs = (
        P("expert", None),
        P("expert", None),
        P("expert", None),
        P("expert", None, "vocab"),
        P("expert", None, "vocab"),
        P("expert", "vocab", None),
        P(),
        P(None, ("expert", "vocab")),
        P("expert"),
    )
    return jax.shard_map(body, mesh=mesh, in_specs=in_specs, out_specs=P("expert"), check_vma=False)
```

time: 553 us -> 160 us (0.29)
  waiting for transfers between devices: 221 us -> 0 us
  blocking collectives: 175 us -> 0 us
  Pallas kernels: 0 us -> 159 us
  matrix products: 41.4 us -> 0 us
  other arithmetic: 36.7 us -> 0 us
  local copies, waits for them, and re-layouts: 36.7 us -> 1.19 us
  starting transfers between devices: 28.1 us -> 0 us
  between operations: 13.6 us -> 0.01 us
    all_to_all x5 -> x0, waiting for transfers between devices: 173 us -> none  [the longest x2 158 us: several_exchanges(): lax.all_to_all(share, axis, split_axis=0, concat_axis=0, tiled=True)]
    pallas_call x0 -> x1, Pallas kernels: none -> 159 us  [body(): pl.pallas_call(kernel, out_shape=jax.ShapeDtypeStruct((1, 128), F32), in_...]
    all_to_all x3 -> x0, blocking collectives: 138 us -> none  [the longest x1 81.5 us: body(): lax.all_to_all(packed, 'expert', split_axis=0, concat_axis=0, tiled=True)]
    all_gather x1 -> x0, waiting for transfers between devices: 47.4 us -> none  [body(): rows = lax.all_gather(normed, 'expert', axis=0, tiled=True)]
    dot_general x4 -> x0, matrix products: 41.4 us -> none  [the longest x1 20.1 us: body(): logits = jnp.dot(rows, lm_weight, preferred_element_type=jnp.float32)]
    all_gather x1 -> x0, blocking collectives: 37.4 us -> none  [body(): row_targets = lax.all_gather(targets, 'expert', axis=0, tiled=True)]
    all_to_all x5 -> x0, starting transfers between devices: 28 us -> none  [the longest x2 11.7 us: several_exchanges(): lax.all_to_all(share, axis, split_axis=0, concat_axis=0, tiled=True)]
    gather x2 -> x0, local copies, waits for them, and re-layouts: 19.6 us -> none  [body(): jnp.take(flat_back, target_rows.reshape(-1), axis=0)]
  transfers between devices with their start and end apart: 6 -> 0, of which waited for: 6 -> 0; matrix products, arithmetic and copies ran while one was open for 2% -> 0% of each run, Pallas kernels for 0% -> 0%
where the time goes in v2:
time: 160 us
  Pallas kernels  159 us (99%)
    pallas_call x1, Pallas kernels, body(): pl.pallas_call(kernel, out_shape=jax.ShapeDtypeStruct((1, 128), F32), in_...  159 us

profile of v2, /device:TPU:0, one launch (start us, length us, event | category | flops | bytes accessed | tf_op | source)
XLA Modules:
  0.0 160.0 jit_solution(2123461122766047878)
XLA Ops:
  0.0 158.8 %layer.1 = f32[1,128]{1,0:T(1,128)} custom-call(bf16[128,2048]{1,0:T(8,128)(2,1)} %tok.1, s32[6,128]{1,0:T(8,128)} %bitcast.10, f32[6,128]{1,0:T(8,128)} %bitcast.11, s32[1,128]{1,0:T(1,128)} %bitcast.12, bf16[2,352,2048]{2,1,0:T(8,128)(2,1)} %bitcast.7, bf16[2,352,2048]{2,1,0:T(8,128)(2,1)} %bitcast.8, bf16[2,352,2048]{2,1,0:T(8,128)(2,1)} %wd.1, ...), custom_call_target="tpu_custom_call" | custom-call | tf_op jit(solution)/shard_map/layer/pallas_call | solution.py:528
  158.8 1.2 copy.11

commit v3 on v2

--- a/solution.py
+++ b/solution.py
@@ -109,40 +109,40 @@
         second[n].start()
         if n < 2:
             third[n][OWN].start()
-    third[2][OWN].start()
-    for n in (0, 2):
-        ring = second[n]
-        ring.copy(0, ring.left, None, ring.right).wait_recv()
-        ring.copy(2, ring.left, 0, ring.right).start()
-        third[n][LEFT].start()
-        ring.copy(1, ring.right, None, ring.left).wait_recv()
-        ring.copy(2, ring.right, 1, ring.left).start()
-        if n == 2:
-            third[n][RIGHT].start()
+    second[0].forward()
+    third[0][LEFT].start()
     third[1][OWN].forward()
     third[0][OWN].forward()
+    second[2].forward()
     second[1].forward()
     third[1][LEFT].start()
+    third[1][RIGHT].start()
+    for j in (OWN, LEFT, RIGHT):
+        third[2][j].start()
+    third[0][LEFT].forward()
     third[0][RIGHT].start()
-    third[1][RIGHT].start()
-    third[2][OWN].forward()
-    for n in (0, 2, 1):
-        second[n].finish()
+    second[0].finish()
+    third[0][FAR].start()
+    second[1].finish()
+    second[2].finish()
     third[2][FAR].start()
-    for n in (0, 1):
-        third[n][LEFT].forward()
-        third[n][FAR].start()
-    for j in (LEFT, RIGHT):
-        third[2][j].forward()
     idle()
     for n in (0, 1):
         third[n][OWN].finish()
-    third[2][FAR].forward()
-    group(OWN)
-    for n in (0, 1):
+
+    def left_on():
+        third[1][LEFT].forward()
+        third[1][FAR].start()
+        third[2][OWN].forward()
+
+    group(OWN, left_on)
+    third[2][LEFT].forward()
+    for n in (1, 0):
         third[n][RIGHT].forward()
+    third[2][RIGHT].forward()
     for n in (0, 1):
         third[n][LEFT].finish()
+    third[2][FAR].forward()
 
     def far_on():
         for n in (0, 1):
@@ -379,6 +379,8 @@
 
     def experts(j, half_way=None):
         if j not in (LEFT, FAR):
+            if half_way:
+                half_way()
             return
         pair = (OWN, LEFT) if j == LEFT else (RIGHT, FAR)
         ys = [shift(co, "y", GROUPS[k]) for k in pair]
@@ -397,6 +399,15 @@
         lax.fori_loop(0, 4, select, 0)
 
         def ffn(l, _):
+            @pl.when(l == 2)
+            def _():
+                if j == LEFT:
+                    half_way()
+                else:
+                    for n in (0, 1):
+                        sc_first[n][OWN].forward()
+                        sc_first[n][LEFT].forward()
+
             both = lax.dot_general(rows[l], vgu[l], (((1,), (1,)), ((), ())), preferred_element_type=F32)
             gate, up = both[:, 0:352], both[:, 352:704]
             hidden = (gate / (1.0 + jnp.exp(-gate)) * up).astype(BF)
@@ -404,14 +415,7 @@
             rows[l] = (jnp.dot(hidden, vd[l], preferred_element_type=F32) * scale).astype(BF)
             return 0
 
-        lax.fori_loop(0, 2, ffn, 0)
-        if j == LEFT:
-            half_way()
-        else:
-            for n in (0, 1):
-                sc_first[n][OWN].forward()
-                sc_first[n][LEFT].forward()
-        lax.fori_loop(2, 4, ffn, 0)
+        lax.fori_loop(0, 4, ffn, 0)
 
         def combine(t, _):
             y, i = place_of(t)
@@ -465,6 +469,9 @@
         y = shift(co, "y", GROUPS[j])
 
         def pair(i, _):
+            if half_way:
+                pl.when(i == 1)(half_way)
+
             lane = lax.broadcasted_iota(jnp.int32, (128, 128), 1)
             column = lax.broadcasted_iota(jnp.int32, (256, 768), 1)
             two = buf[y, pl.ds(2 * i, 2)].reshape(256, 2048)
@@ -484,12 +491,7 @@
                 stats[q + s] = jnp.transpose(both)[0:2]
             return 0
 
-        if half_way is None:
-            lax.fori_loop(0, 2, pair, 0)
-        else:
-            lax.fori_loop(0, 1, pair, 0)
-            half_way()
-            lax.fori_loop(1, 2, pair, 0)
+        lax.fori_loop(0, 2, pair, 0)
 
     def note(j, i):
         y, z, x = shift(co, "y", GROUPS[j]), (co["z"] + i // 4) % 4, (co["x"] + i) % 4

time: 160 us -> 152 us (0.950)
  Pallas kernels: 159 us -> 151 us
    pallas_call x1, Pallas kernels: 159 us -> 151 us  [body(): pl.pallas_call(kernel, out_shape=jax.ShapeDtypeStruct((1, 128), F32), in_...]
where the time goes in v3:
time: 152 us
  Pallas kernels  151 us (99%)
    pallas_call x1, Pallas kernels, body(): pl.pallas_call(kernel, out_shape=jax.ShapeDtypeStruct((1, 128), F32), in_...  151 us

profile of v3, /device:TPU:0, one launch (start us, length us, event | category | flops | bytes accessed | tf_op | source)
XLA Modules:
  0.0 151.8 jit_solution(10815769209918455925)
XLA Ops:
  0.0 150.6 %layer.1 = f32[1,128]{1,0:T(1,128)} custom-call(bf16[128,2048]{1,0:T(8,128)(2,1)} %tok.1, s32[6,128]{1,0:T(8,128)} %bitcast.10, f32[6,128]{1,0:T(8,128)} %bitcast.11, s32[1,128]{1,0:T(1,128)} %bitcast.12, bf16[2,352,2048]{2,1,0:T(8,128)(2,1)} %bitcast.7, bf16[2,352,2048]{2,1,0:T(8,128)(2,1)} %bitcast.8, bf16[2,352,2048]{2,1,0:T(8,128)(2,1)} %wd.1, ...), custom_call_target="tpu_custom_call" | custom-call | tf_op jit(solution)/shard_map/layer/pallas_call | solution.py:530
  150.6 1.2 copy.11

commit v4 on v3

--- a/solution.py
+++ b/solution.py
@@ -406,6 +406,12 @@
                 else:
                     for n in (0, 1):
                         sc_first[n][OWN].forward()
+
+            if j == FAR:
+
+                @pl.when(l == 3)
+                def _():
+                    for n in (0, 1):
                         sc_first[n][LEFT].forward()
 
             both = lax.dot_general(rows[l], vgu[l], (((1,), (1,)), ((), ())), preferred_element_type=F32)

time: 152 us -> 152 us (level)
  no operation moved by 1% of the time
where the time goes in v4:
time: 152 us
  Pallas kernels  151 us (99%)
    pallas_call x1, Pallas kernels, body(): pl.pallas_call(kernel, out_shape=jax.ShapeDtypeStruct((1, 128), F32), in_...  151 us

profile of v4, /device:TPU:0, one launch (start us, length us, event | category | flops | bytes accessed | tf_op | source)
XLA Modules:
  0.0 151.8 jit_solution(1235591566287828142)
XLA Ops:
  0.0 150.6 %layer.1 = f32[1,128]{1,0:T(1,128)} custom-call(bf16[128,2048]{1,0:T(8,128)(2,1)} %tok.1, s32[6,128]{1,0:T(8,128)} %bitcast.10, f32[6,128]{1,0:T(8,128)} %bitcast.11, s32[1,128]{1,0:T(1,128)} %bitcast.12, bf16[2,352,2048]{2,1,0:T(8,128)(2,1)} %bitcast.7, bf16[2,352,2048]{2,1,0:T(8,128)(2,1)} %bitcast.8, bf16[2,352,2048]{2,1,0:T(8,128)(2,1)} %wd.1, ...), custom_call_target="tpu_custom_call" | custom-call | tf_op jit(solution)/shard_map/layer/pallas_call | solution.py:536
  150.6 1.2 copy.11
